TPU v7x, 128 devices: a whole 4x4x4 slice. The times are simulated.
128 devices in a mesh: tiles: 16 (over y, z), lag: 8 (over x, core).
Axes of the slice: x: 4, y: 4, z: 4, core: 2. Of those that a mesh axis runs over, the one named last changes fastest.
Arguments:
- spectra: bfloat16 [32, 2, 2, 128, 8192], P('tiles', None, None, None, 'lag'), may hold values from -6 to 6
- requests: int32 [16, 6], replicated, may hold values from 0 to 31, as said below
- pairs: int32 [16, 3, 2], P('tiles'), may hold values from 0 to 5, as said below
- counts: int32 [16], P('tiles'), may hold values from 2 to 3, as said below
Outputs:
- stacked_lags: float32 [48, 64, 128, 128], P('tiles', 'lag')
Inputs may be any that keep to these rules, and one draw needn't show every extreme that they name: Block b is held by index b // 2 of tiles; each row of requests names 6 blocks held by 6 different indices. Each row's 3 entries are pairs (i, j) of request slots with i < j that together use every request slot once. The first counts[d] slots of row d are live, the others give zeros; some index has 3.
All inputs are finite; a program needn't handle non-finite values.
Results may differ from a plain program's by a relative error of at most 0.012.
Values may be sent and summed in bfloat16 or wider, within the bound.
A program may use at most 128 MiB of HBM per device.

v0:
```python
import math
import jax
import jax.numpy as jnp
from jax import lax
from jax.sharding import PartitionSpec as P

F = 8192
W = 2
LAGS = 64
FBLK = 128


def phase_table(freq_first, width):
    frequencies = freq_first + jnp.arange(width, dtype=jnp.int32)
    shifts = (jnp.arange(LAGS, dtype=jnp.int32) - LAGS // 2) % F
    phase_index = frequencies[:, None] * shifts[None, :] % F
    angles = phase_index.astype(jnp.float32) * (2.0 * math.pi / F)
    return jnp.concatenate([jnp.cos(angles), -jnp.sin(angles)], axis=0).astype(jnp.bfloat16)


def cross_block(left_part, right_part):
    left_wide = left_part.astype(jnp.float32)
    right_wide = right_part.astype(jnp.float32)
    real_part = jnp.sum(
        left_wide[:, 0, :, None, :] * right_wide[:, 0, None, :, :]
        + left_wide[:, 1, :, None, :] * right_wide[:, 1, None, :, :],
        axis=0,
    )
    imag_part = jnp.sum(
        left_wide[:, 1, :, None, :] * right_wide[:, 0, None, :, :]
        - left_wide[:, 0, :, None, :] * right_wide[:, 1, None, :, :],
        axis=0,
    )
    channels = left_part.shape[2]
    return (
        jnp.concatenate([real_part, imag_part], axis=-1)
        .reshape(channels * channels, -1)
        .astype(jnp.bfloat16)
    )


def band_sum(left_block, right_block, band_first):
    channels = left_block.shape[2]
    block_count = left_block.shape[-1] // FBLK

    def block_step(running, block_index):
        offset = block_index * FBLK
        left_part = lax.dynamic_slice_in_dim(left_block, offset, FBLK, 3)
        right_part = lax.dynamic_slice_in_dim(right_block, offset, FBLK, 3)
        stacked = cross_block(left_part, right_part)
        phases = phase_table(band_first + offset, FBLK)
        return (
            running
            + lax.dot_general(
                phases, stacked, (((0,), (1,)), ((), ())), preferred_element_type=jnp.float32
            ),
            None,
        )

    running = jnp.zeros((LAGS, channels * channels), jnp.float32)
    running, unused = lax.scan(block_step, running, jnp.arange(block_count, dtype=jnp.int32))
    return running


def per_device(spectra, requests, pairs, counts):
    channels = spectra.shape[3]
    own_index = lax.axis_index("tiles")
    wanted = lax.dynamic_index_in_dim(requests, own_index, 0, keepdims=False)
    empty = jnp.zeros((wanted.shape[0],) + spectra.shape[1:], jnp.bfloat16)
    shards = lax.all_gather(spectra, "tiles", axis=0, tiled=True)
    inside = (wanted >= 0) & (wanted < shards.shape[0])
    taken = jnp.take(shards, jnp.clip(wanted, 0, shards.shape[0] - 1), axis=0)
    needed = jnp.where(inside[:, None, None, None, None], taken, empty)
    band_first = lax.axis_index("lag") * spectra.shape[-1]
    norm_factor = 1.0 / math.sqrt(2.0 * W * F)
    live_count = counts[0]
    tile_pairs = pairs[0]
    slot_total = tile_pairs.shape[0]
    terms = []
    for slot_index in range(slot_total):
        left_block = jnp.take(needed, tile_pairs[slot_index, 0], axis=0)
        right_block = jnp.take(needed, tile_pairs[slot_index, 1], axis=0)
        result = band_sum(left_block, right_block, band_first) * norm_factor
        terms.append(jnp.where(slot_index < live_count, result, jnp.zeros_like(result)))
    partial_terms = jnp.stack(terms).reshape(slot_total, LAGS, channels, channels)
    return lax.psum_scatter(
        partial_terms.astype(jnp.bfloat16), "lag", scatter_dimension=1, tiled=True
    ).astype(jnp.float32)


def solution(mesh):
    placed = (P("tiles", None, None, None, "lag"), P(), P("tiles", None, None), P("tiles"))
    return jax.shard_map(
        per_device,
        mesh=mesh,
        in_specs=placed,
        out_specs=P("tiles", "lag", None, None),
        check_vma=False,
    )
```

profile of v0, /device:TPU:1, one launch (start us, length us, event | category | flops | bytes accessed | tf_op | source)
XLA Modules:
  0.0 1019.2 jit_solution(7977212312652234884)
XLA Ops:
  22.7 187.3 %all-gather.2.cloned.1.call-done = bf16[32,2,2,128,1024]{4,3,2,1,0:T(8,128)(2,1)} async-done(((bf16[2,2,2,128,1024]{4,3,2,1,0:T(8,128)(2,1)}), bf16[32,2,2,128,1024]{4,3,2,1,0:T(8,128)(2,1)}) %all-gather.2.cloned.1.call-update) | async-done | bytes 33554448 | tf_op jit(solution)/shard_map/all_gather | solution.py:70
  221.3 236.1 %while.40 = (s32[]{:T(128)}, f32[64,16384]{1,0:T(8,128)}, s32[8]{0:T(128)S(1)}, s32[]{:T(128)}, bf16[2,2,128,1024]{3,2,1,0:T(8,128)(2,1)S(1)}, /*index=5*/bf16[2...) while((s32[]{:T(128)}, f32[64,16384]{1,0:T(8,128)}, ...), condition=%wide.region_3.5_spmd.clone, body=%wide.region_0.0_spmd.clone.sunk | while | flops 585442176 | bytes 44893884 | solution.py:61
  222.8 11.7 %add_reduce_fusion.6 = (bf16[128,128,128]{2,1,0:T(8,128)(2,1)S(1)}, bf16[128,128,128]{2,1,0:T(8,128)(2,1)}) fusion(f32[2,128,128]{2,1,0:T(8,128)S(1)} %get-tuple-element.564, f32[2,128,128]{2,1,0:T(8,128)S(1)} %get-tuple-element.566, f32[2,128,128]{2,1,0:T(8,128)S(1)} %get-tuple-element.567, f32[2,128,128]{2,1,0:T(8,128)S(1)} %get-tuple-element.568), kind=kLoop, calls=%fused_computation.3.clone.1 | loop fusion | flops 29360128 | bytes 8912896 | tf_op jit(solution)/shard_map/while/body/eval_jaxpr/reduce_sum | solution.py:24
  251.3 11.7 %add_reduce_fusion.6 = (bf16[128,128,128]{2,1,0:T(8,128)(2,1)S(1)}, bf16[128,128,128]{2,1,0:T(8,128)(2,1)}) fusion(f32[2,128,128]{2,1,0:T(8,128)S(1)} %get-tuple-element.564, f32[2,128,128]{2,1,0:T(8,128)S(1)} %get-tuple-element.566, f32[2,128,128]{2,1,0:T(8,128)S(1)} %get-tuple-element.567, f32[2,128,128]{2,1,0:T(8,128)S(1)} %get-tuple-element.568), kind=kLoop, calls=%fused_computation.3.clone.1 | loop fusion | flops 29360128 | bytes 8912896 | tf_op jit(solution)/shard_map/while/body/eval_jaxpr/reduce_sum | solution.py:24
  310.6 11.7 %add_reduce_fusion.6 = (bf16[128,128,128]{2,1,0:T(8,128)(2,1)S(1)}, bf16[128,128,128]{2,1,0:T(8,128)(2,1)}) fusion(f32[2,128,128]{2,1,0:T(8,128)S(1)} %get-tuple-element.564, f32[2,128,128]{2,1,0:T(8,128)S(1)} %get-tuple-element.566, f32[2,128,128]{2,1,0:T(8,128)S(1)} %get-tuple-element.567, f32[2,128,128]{2,1,0:T(8,128)S(1)} %get-tuple-element.568), kind=kLoop, calls=%fused_computation.3.clone.1 | loop fusion | flops 29360128 | bytes 8912896 | tf_op jit(solution)/shard_map/while/body/eval_jaxpr/reduce_sum | solution.py:24
  340.2 11.7 %add_reduce_fusion.6 = (bf16[128,128,128]{2,1,0:T(8,128)(2,1)S(1)}, bf16[128,128,128]{2,1,0:T(8,128)(2,1)}) fusion(f32[2,128,128]{2,1,0:T(8,128)S(1)} %get-tuple-element.564, f32[2,128,128]{2,1,0:T(8,128)S(1)} %get-tuple-element.566, f32[2,128,128]{2,1,0:T(8,128)S(1)} %get-tuple-element.567, f32[2,128,128]{2,1,0:T(8,128)S(1)} %get-tuple-element.568), kind=kLoop, calls=%fused_computation.3.clone.1 | loop fusion | flops 29360128 | bytes 8912896 | tf_op jit(solution)/shard_map/while/body/eval_jaxpr/reduce_sum | solution.py:24
  369.9 11.7 %add_reduce_fusion.6 = (bf16[128,128,128]{2,1,0:T(8,128)(2,1)S(1)}, bf16[128,128,128]{2,1,0:T(8,128)(2,1)}) fusion(f32[2,128,128]{2,1,0:T(8,128)S(1)} %get-tuple-element.564, f32[2,128,128]{2,1,0:T(8,128)S(1)} %get-tuple-element.566, f32[2,128,128]{2,1,0:T(8,128)S(1)} %get-tuple-element.567, f32[2,128,128]{2,1,0:T(8,128)S(1)} %get-tuple-element.568), kind=kLoop, calls=%fused_computation.3.clone.1 | loop fusion | flops 29360128 | bytes 8912896 | tf_op jit(solution)/shard_map/while/body/eval_jaxpr/reduce_sum | solution.py:24
  399.5 11.7 %add_reduce_fusion.6 = (bf16[128,128,128]{2,1,0:T(8,128)(2,1)S(1)}, bf16[128,128,128]{2,1,0:T(8,128)(2,1)}) fusion(f32[2,128,128]{2,1,0:T(8,128)S(1)} %get-tuple-element.564, f32[2,128,128]{2,1,0:T(8,128)S(1)} %get-tuple-element.566, f32[2,128,128]{2,1,0:T(8,128)S(1)} %get-tuple-element.567, f32[2,128,128]{2,1,0:T(8,128)S(1)} %get-tuple-element.568), kind=kLoop, calls=%fused_computation.3.clone.1 | loop fusion | flops 29360128 | bytes 8912896 | tf_op jit(solution)/shard_map/while/body/eval_jaxpr/reduce_sum | solution.py:24
  460.7 244.2 %while.41 = (s32[]{:T(128)}, f32[64,16384]{1,0:T(8,128)}, s32[8]{0:T(128)S(1)}, s32[]{:T(128)}, bf16[2,2,128,1024]{3,2,1,0:T(8,128)(2,1)}, /*index=5*/bf16[2,2,1...) while((s32[]{:T(128)}, f32[64,16384]{1,0:T(8,128)}, s32[8]{0:T(128)S(1)}, ...), condition=%wide.region_7.9_spmd.clone, body=%wide.region_4.8_spmd.clone.sunk | while | flops 585442176 | bytes 44893884 | solution.py:61
  463.2 11.7 %add_reduce_fusion.7 = (bf16[128,128,128]{2,1,0:T(8,128)(2,1)S(1)}, bf16[128,128,128]{2,1,0:T(8,128)(2,1)}) fusion(f32[2,128,128]{2,1,0:T(8,128)S(1)} %get-tuple-element.580, f32[2,128,128]{2,1,0:T(8,128)S(1)} %get-tuple-element.582, f32[2,128,128]{2,1,0:T(8,128)S(1)} %get-tuple-element.583, f32[2,128,128]{2,1,0:T(8,128)S(1)} %get-tuple-element.584), kind=kLoop, calls=%fused_computation.34.clone.1 | loop fusion | flops 29360128 | bytes 8912896 | tf_op jit(solution)/shard_map/while/body/eval_jaxpr/reduce_sum | solution.py:24
  492.7 11.7 %add_reduce_fusion.7 = (bf16[128,128,128]{2,1,0:T(8,128)(2,1)S(1)}, bf16[128,128,128]{2,1,0:T(8,128)(2,1)}) fusion(f32[2,128,128]{2,1,0:T(8,128)S(1)} %get-tuple-element.580, f32[2,128,128]{2,1,0:T(8,128)S(1)} %get-tuple-element.582, f32[2,128,128]{2,1,0:T(8,128)S(1)} %get-tuple-element.583, f32[2,128,128]{2,1,0:T(8,128)S(1)} %get-tuple-element.584), kind=kLoop, calls=%fused_computation.34.clone.1 | loop fusion | flops 29360128 | bytes 8912896 | tf_op jit(solution)/shard_map/while/body/eval_jaxpr/reduce_sum | solution.py:24
  523.3 11.7 %add_reduce_fusion.7 = (bf16[128,128,128]{2,1,0:T(8,128)(2,1)S(1)}, bf16[128,128,128]{2,1,0:T(8,128)(2,1)}) fusion(f32[2,128,128]{2,1,0:T(8,128)S(1)} %get-tuple-element.580, f32[2,128,128]{2,1,0:T(8,128)S(1)} %get-tuple-element.582, f32[2,128,128]{2,1,0:T(8,128)S(1)} %get-tuple-element.583, f32[2,128,128]{2,1,0:T(8,128)S(1)} %get-tuple-element.584), kind=kLoop, calls=%fused_computation.34.clone.1 | loop fusion | flops 29360128 | bytes 8912896 | tf_op jit(solution)/shard_map/while/body/eval_jaxpr/reduce_sum | solution.py:24
  554.0 11.7 %add_reduce_fusion.7 = (bf16[128,128,128]{2,1,0:T(8,128)(2,1)S(1)}, bf16[128,128,128]{2,1,0:T(8,128)(2,1)}) fusion(f32[2,128,128]{2,1,0:T(8,128)S(1)} %get-tuple-element.580, f32[2,128,128]{2,1,0:T(8,128)S(1)} %get-tuple-element.582, f32[2,128,128]{2,1,0:T(8,128)S(1)} %get-tuple-element.583, f32[2,128,128]{2,1,0:T(8,128)S(1)} %get-tuple-element.584), kind=kLoop, calls=%fused_computation.34.clone.1 | loop fusion | flops 29360128 | bytes 8912896 | tf_op jit(solution)/shard_map/while/body/eval_jaxpr/reduce_sum | solution.py:24
  615.3 11.7 %add_reduce_fusion.7 = (bf16[128,128,128]{2,1,0:T(8,128)(2,1)S(1)}, bf16[128,128,128]{2,1,0:T(8,128)(2,1)}) fusion(f32[2,128,128]{2,1,0:T(8,128)S(1)} %get-tuple-element.580, f32[2,128,128]{2,1,0:T(8,128)S(1)} %get-tuple-element.582, f32[2,128,128]{2,1,0:T(8,128)S(1)} %get-tuple-element.583, f32[2,128,128]{2,1,0:T(8,128)S(1)} %get-tuple-element.584), kind=kLoop, calls=%fused_computation.34.clone.1 | loop fusion | flops 29360128 | bytes 8912896 | tf_op jit(solution)/shard_map/while/body/eval_jaxpr/reduce_sum | solution.py:24
  645.9 11.7 %add_reduce_fusion.7 = (bf16[128,128,128]{2,1,0:T(8,128)(2,1)S(1)}, bf16[128,128,128]{2,1,0:T(8,128)(2,1)}) fusion(f32[2,128,128]{2,1,0:T(8,128)S(1)} %get-tuple-element.580, f32[2,128,128]{2,1,0:T(8,128)S(1)} %get-tuple-element.582, f32[2,128,128]{2,1,0:T(8,128)S(1)} %get-tuple-element.583, f32[2,128,128]{2,1,0:T(8,128)S(1)} %get-tuple-element.584), kind=kLoop, calls=%fused_computation.34.clone.1 | loop fusion | flops 29360128 | bytes 8912896 | tf_op jit(solution)/shard_map/while/body/eval_jaxpr/reduce_sum | solution.py:24
  676.6 11.7 %add_reduce_fusion.7 = (bf16[128,128,128]{2,1,0:T(8,128)(2,1)S(1)}, bf16[128,128,128]{2,1,0:T(8,128)(2,1)}) fusion(f32[2,128,128]{2,1,0:T(8,128)S(1)} %get-tuple-element.580, f32[2,128,128]{2,1,0:T(8,128)S(1)} %get-tuple-element.582, f32[2,128,128]{2,1,0:T(8,128)S(1)} %get-tuple-element.583, f32[2,128,128]{2,1,0:T(8,128)S(1)} %get-tuple-element.584), kind=kLoop, calls=%fused_computation.34.clone.1 | loop fusion | flops 29360128 | bytes 8912896 | tf_op jit(solution)/shard_map/while/body/eval_jaxpr/reduce_sum | solution.py:24
  709.5 243.4 %while.42 = (s32[]{:T(128)}, f32[64,16384]{1,0:T(8,128)}, s32[8]{0:T(128)S(1)}, s32[]{:T(128)}, bf16[2,2,128,1024]{3,2,1,0:T(8,128)(2,1)}, /*index=5*/bf16[2,2,1...) while((s32[]{:T(128)}, f32[64,16384]{1,0:T(8,128)}, s32[8]{0:T(128)S(1)}, ...), condition=%wide.region_11.13_spmd.clone, body=%wide.region_8.12_spmd.clone.sunk | while | flops 585442176 | bytes 44893884 | solution.py:61
  711.9 11.7 %add_reduce_fusion.8 = (bf16[128,128,128]{2,1,0:T(8,128)(2,1)S(1)}, bf16[128,128,128]{2,1,0:T(8,128)(2,1)}) fusion(f32[2,128,128]{2,1,0:T(8,128)S(1)} %get-tuple-element.596, f32[2,128,128]{2,1,0:T(8,128)S(1)} %get-tuple-element.598, f32[2,128,128]{2,1,0:T(8,128)S(1)} %get-tuple-element.599, f32[2,128,128]{2,1,0:T(8,128)S(1)} %get-tuple-element.600), kind=kLoop, calls=%fused_computation.65.clone.1 | loop fusion | flops 29360128 | bytes 8912896 | tf_op jit(solution)/shard_map/while/body/eval_jaxpr/reduce_sum | solution.py:24
  802.4 11.7 %add_reduce_fusion.8 = (bf16[128,128,128]{2,1,0:T(8,128)(2,1)S(1)}, bf16[128,128,128]{2,1,0:T(8,128)(2,1)}) fusion(f32[2,128,128]{2,1,0:T(8,128)S(1)} %get-tuple-element.596, f32[2,128,128]{2,1,0:T(8,128)S(1)} %get-tuple-element.598, f32[2,128,128]{2,1,0:T(8,128)S(1)} %get-tuple-element.599, f32[2,128,128]{2,1,0:T(8,128)S(1)} %get-tuple-element.600), kind=kLoop, calls=%fused_computation.65.clone.1 | loop fusion | flops 29360128 | bytes 8912896 | tf_op jit(solution)/shard_map/while/body/eval_jaxpr/reduce_sum | solution.py:24
  833.0 11.7 %add_reduce_fusion.8 = (bf16[128,128,128]{2,1,0:T(8,128)(2,1)S(1)}, bf16[128,128,128]{2,1,0:T(8,128)(2,1)}) fusion(f32[2,128,128]{2,1,0:T(8,128)S(1)} %get-tuple-element.596, f32[2,128,128]{2,1,0:T(8,128)S(1)} %get-tuple-element.598, f32[2,128,128]{2,1,0:T(8,128)S(1)} %get-tuple-element.599, f32[2,128,128]{2,1,0:T(8,128)S(1)} %get-tuple-element.600), kind=kLoop, calls=%fused_computation.65.clone.1 | loop fusion | flops 29360128 | bytes 8912896 | tf_op jit(solution)/shard_map/while/body/eval_jaxpr/reduce_sum | solution.py:24
  863.6 11.7 %add_reduce_fusion.8 = (bf16[128,128,128]{2,1,0:T(8,128)(2,1)S(1)}, bf16[128,128,128]{2,1,0:T(8,128)(2,1)}) fusion(f32[2,128,128]{2,1,0:T(8,128)S(1)} %get-tuple-element.596, f32[2,128,128]{2,1,0:T(8,128)S(1)} %get-tuple-element.598, f32[2,128,128]{2,1,0:T(8,128)S(1)} %get-tuple-element.599, f32[2,128,128]{2,1,0:T(8,128)S(1)} %get-tuple-element.600), kind=kLoop, calls=%fused_computation.65.clone.1 | loop fusion | flops 29360128 | bytes 8912896 | tf_op jit(solution)/shard_map/while/body/eval_jaxpr/reduce_sum | solution.py:24
  894.1 11.7 %add_reduce_fusion.8 = (bf16[128,128,128]{2,1,0:T(8,128)(2,1)S(1)}, bf16[128,128,128]{2,1,0:T(8,128)(2,1)}) fusion(f32[2,128,128]{2,1,0:T(8,128)S(1)} %get-tuple-element.596, f32[2,128,128]{2,1,0:T(8,128)S(1)} %get-tuple-element.598, f32[2,128,128]{2,1,0:T(8,128)S(1)} %get-tuple-element.599, f32[2,128,128]{2,1,0:T(8,128)S(1)} %get-tuple-element.600), kind=kLoop, calls=%fused_computation.65.clone.1 | loop fusion | flops 29360128 | bytes 8912896 | tf_op jit(solution)/shard_map/while/body/eval_jaxpr/reduce_sum | solution.py:24
  924.7 11.7 %add_reduce_fusion.8 = (bf16[128,128,128]{2,1,0:T(8,128)(2,1)S(1)}, bf16[128,128,128]{2,1,0:T(8,128)(2,1)}) fusion(f32[2,128,128]{2,1,0:T(8,128)S(1)} %get-tuple-element.596, f32[2,128,128]{2,1,0:T(8,128)S(1)} %get-tuple-element.598, f32[2,128,128]{2,1,0:T(8,128)S(1)} %get-tuple-element.599, f32[2,128,128]{2,1,0:T(8,128)S(1)} %get-tuple-element.600), kind=kLoop, calls=%fused_computation.65.clone.1 | loop fusion | flops 29360128 | bytes 8912896 | tf_op jit(solution)/shard_map/while/body/eval_jaxpr/reduce_sum | solution.py:24
  967.2 42.6 %reduce-scatter.5.cloned.1.call-done = bf16[8,49152]{1,0:T(8,128)(2,1)} async-done(((bf16[64,49152]{1,0:T(8,128)(2,1)}), bf16[8,49152]{1,0:T(8,128)(2,1)}) %reduce-scatter.5.cloned.1.call-update) | async-done | bytes 786448
  (301 shorter events, 525.5 us)
Async XLA Ops:
  6.5 203.4 %all-gather.2.cloned.1.call-start = ((), (), s32[]{:S(2)}) async-start(), calls=%async_computation.1 | async-start | bytes 35651584 | tf_op jit(solution)/shard_map/all_gather | solution.py:70
  7.3 1002.5 %reduce-scatter.5.cloned.1.call-start = ((), (), s32[]{:S(2)}) async-start(), calls=%async_computation.2 | async-start | bytes 7077888
  952.9 3.5 copy-start
Sparse Core Ops, SparseCore 0:
  9.5 200.4 all-gather.1
  967.3 42.4 reduce-scatter.4
where the time goes:
time: 1020 us
  other arithmetic  475 us (47%)
  waiting for transfers between devices  231 us (23%)
  matrix products  218 us (21%)
  local copies, waits for them, and re-layouts  53.4 us (5%)
  between operations  25.5 us (2%)
  loops' own time  16.6 us (2%)
    reduce_sum x24, other arithmetic, cross_block(): jnp.sum(left_wide[:, 0, :, None, :] * right_wide[:, 0, None, :, :] + left...  280 us
    dot_general x24, matrix products, block_step(): lax.dot_general(phases, stacked, (((0,), (1,)), ((), ())), preferred_elem...  218 us
    all_gather x1, waiting for transfers between devices, per_device(): shards = lax.all_gather(spectra, 'tiles', axis=0, tiled=True)  187 us
    concatenate x24, other arithmetic, cross_block(): jnp.concatenate([real_part, imag_part], axis=-1)  171 us
    unnamed x3, waiting for transfers between devices  43.3 us
  transfers between devices with their start and end apart: 2, of which 2 were waited for; matrix products, arithmetic and copies ran while one was open for 0% of the time, Pallas kernels for 0%

commit v1 on v0

--- a/solution.py
+++ b/solution.py
@@ -8,6 +8,27 @@
 W = 2
 LAGS = 64
 FBLK = 128
+
+
+def collect(array, axis, dim):
+    devices, mine, rows = (lax.axis_size(axis), lax.axis_index(axis), array.shape[dim])
+    ahead = [(i, (i + 1) % devices) for i in range(devices)]
+    behind = [(i, (i - 1) % devices) for i in range(devices)]
+    out = jnp.zeros((*array.shape[:dim], devices * rows, *array.shape[dim + 1 :]), array.dtype)
+    out = lax.dynamic_update_slice_in_dim(out, array, mine * rows, axis=dim)
+    from_left = from_right = array
+    half = devices // 2
+    for step in range(1, half + 1):
+        from_left = lax.ppermute(from_left, axis, ahead)
+        out = lax.dynamic_update_slice_in_dim(
+            out, from_left, (mine - step) % devices * rows, axis=dim
+        )
+        if step < devices - half:
+            from_right = lax.ppermute(from_right, axis, behind)
+            out = lax.dynamic_update_slice_in_dim(
+                out, from_right, (mine + step) % devices * rows, axis=dim
+            )
+    return out
 
 
 def phase_table(freq_first, width):
@@ -67,7 +88,7 @@
     own_index = lax.axis_index("tiles")
     wanted = lax.dynamic_index_in_dim(requests, own_index, 0, keepdims=False)
     empty = jnp.zeros((wanted.shape[0],) + spectra.shape[1:], jnp.bfloat16)
-    shards = lax.all_gather(spectra, "tiles", axis=0, tiled=True)
+    shards = collect(spectra, "tiles", 0)
     inside = (wanted >= 0) & (wanted < shards.shape[0])
     taken = jnp.take(shards, jnp.clip(wanted, 0, shards.shape[0] - 1), axis=0)
     needed = jnp.where(inside[:, None, None, None, None], taken, empty)

time: 1020 us -> 1210 us (1.19)
  waiting for transfers between devices: 231 us -> 332 us
  local copies, waits for them, and re-layouts: 53.4 us -> 101 us
  starting transfers between devices: 0.04 us -> 32 us
    ppermute x0 -> x15, waiting for transfers between devices: none -> 286 us  [the longest x8 284 us: collect(): from_left = lax.ppermute(from_left, axis, ahead)]
    all_gather x1 -> x0, waiting for transfers between devices: 187 us -> none  [per_device(): shards = lax.all_gather(spectra, 'tiles', axis=0, tiled=True)]
    ppermute x0 -> x15, starting transfers between devices: none -> 32 us  [the longest x7 29.5 us: collect(): from_right = lax.ppermute(from_right, axis, behind)]
    dynamic_update_slice x0 -> x16, local copies, waits for them, and re-layouts: none -> 30.7 us  [the longest x8 15.3 us: collect(): lax.dynamic_update_slice_in_dim(out, from_left, (mine - step) % devices *...]
    unnamed x3 -> x2, waiting for transfers between devices: 43.3 us -> 45.3 us
  transfers between devices with their start and end apart: 2 -> 16, of which waited for: 2 -> 10; matrix products, arithmetic and copies ran while one was open for 0% -> 4% of each run, Pallas kernels for 0% -> 0%
where the time goes in v1:
time: 1210 us; the launch traced here: 1200 us
  other arithmetic  477 us (39%)
  waiting for transfers between devices  332 us (27%)
  matrix products  217 us (18%)
  local copies, waits for them, and re-layouts  101 us (8%)
  starting transfers between devices  32 us (3%)
  between operations  25.6 us (2%)
  loops' own time  17.3 us (1%)
    ppermute x8, waiting for transfers between devices, collect(): from_left = lax.ppermute(from_left, axis, ahead)  284 us
    reduce_sum x24, other arithmetic, cross_block(): jnp.sum(left_wide[:, 0, :, None, :] * right_wide[:, 0, None, :, :] + left...  280 us
    dot_general x24, matrix products, block_step(): lax.dot_general(phases, stacked, (((0,), (1,)), ((), ())), preferred_elem...  217 us
    concatenate x24, other arithmetic, cross_block(): jnp.concatenate([real_part, imag_part], axis=-1)  172 us
    unnamed x2, waiting for transfers between devices  45.3 us
    ppermute x7, starting transfers between devices, collect(): from_right = lax.ppermute(from_right, axis, behind)  29.5 us
  transfers between devices with their start and end apart: 16, of which 10 were waited for; matrix products, arithmetic and copies ran while one was open for 4% of the time, Pallas kernels for 0%

profile of v1, /device:TPU:1, one launch (start us, length us, event | category | flops | bytes accessed | tf_op | source)
XLA Modules:
  0.0 1202.2 jit_solution(11175479433987839671)
XLA Ops:
  13.6 45.6 %collective-permute-done = bf16[2,2,2,128,1024]{4,3,2,1,0:T(8,128)(2,1)S(1)} collective-permute-done((bf16[2,2,2,128,1024]{4,3,2,1,0:T(8,128)(2,1)}, bf16[2,2,2,128,1024]{4,3,2,1,0:T(8,128)(2,1)S(1)}, u32[]{:S(2)}, u32[]{:S(2)}) %collective-permute-start) | collective-permute-done | bytes 2097184 | tf_op jit(solution)/shard_map/ppermute | solution.py:22
  63.9 44.4 %collective-permute-done.2 = bf16[2,2,2,128,1024]{4,3,2,1,0:T(8,128)(2,1)S(1)} collective-permute-done((bf16[2,2,2,128,1024]{4,3,2,1,0:T(8,128)(2,1)S(1)}, bf16[2,2,2,128,1024]{4,3,2,1,0:T(8,128)(2,1)S(1)}, u32[]{:S(2)}, u32[]{:S(2)}) %collective-permute-start.2) | collective-permute-done | bytes 2097184 | tf_op jit(solution)/shard_map/ppermute | solution.py:22
  113.2 43.4 %collective-permute-done.4 = bf16[2,2,2,128,1024]{4,3,2,1,0:T(8,128)(2,1)S(1)} collective-permute-done((bf16[2,2,2,128,1024]{4,3,2,1,0:T(8,128)(2,1)S(1)}, bf16[2,2,2,128,1024]{4,3,2,1,0:T(8,128)(2,1)S(1)}, u32[]{:S(2)}, u32[]{:S(2)}) %collective-permute-start.4) | collective-permute-done | bytes 2097184 | tf_op jit(solution)/shard_map/ppermute | solution.py:22
  161.5 42.5 %collective-permute-done.6 = bf16[2,2,2,128,1024]{4,3,2,1,0:T(8,128)(2,1)S(1)} collective-permute-done((bf16[2,2,2,128,1024]{4,3,2,1,0:T(8,128)(2,1)S(1)}, bf16[2,2,2,128,1024]{4,3,2,1,0:T(8,128)(2,1)S(1)}, u32[]{:S(2)}, u32[]{:S(2)}) %collective-permute-start.6) | collective-permute-done | bytes 2097184 | tf_op jit(solution)/shard_map/ppermute | solution.py:22
  208.9 41.6 %collective-permute-done.8 = bf16[2,2,2,128,1024]{4,3,2,1,0:T(8,128)(2,1)S(1)} collective-permute-done((bf16[2,2,2,128,1024]{4,3,2,1,0:T(8,128)(2,1)S(1)}, bf16[2,2,2,128,1024]{4,3,2,1,0:T(8,128)(2,1)S(1)}, u32[]{:S(2)}, u32[]{:S(2)}) %collective-permute-start.8) | collective-permute-done | bytes 2097184 | tf_op jit(solution)/shard_map/ppermute | solution.py:22
  255.3 40.8 %collective-permute-done.10 = bf16[2,2,2,128,1024]{4,3,2,1,0:T(8,128)(2,1)} collective-permute-done((bf16[2,2,2,128,1024]{4,3,2,1,0:T(8,128)(2,1)S(1)}, bf16[2,2,2,128,1024]{4,3,2,1,0:T(8,128)(2,1)}, u32[]{:S(2)}, u32[]{:S(2)}) %collective-permute-start.10) | collective-permute-done | bytes 2097184 | tf_op jit(solution)/shard_map/ppermute | solution.py:22
  369.8 15.2 %collective-permute-done.14 = bf16[2,2,2,128,1024]{4,3,2,1,0:T(8,128)(2,1)S(1)} collective-permute-done((bf16[2,2,2,128,1024]{4,3,2,1,0:T(8,128)(2,1)}, bf16[2,2,2,128,1024]{4,3,2,1,0:T(8,128)(2,1)S(1)}, u32[]{:S(2)}, u32[]{:S(2)}) %collective-permute-start.14) | collective-permute-done | bytes 2097184 | tf_op jit(solution)/shard_map/ppermute | solution.py:22
  399.5 237.0 %while.40 = (s32[]{:T(128)}, f32[64,16384]{1,0:T(8,128)}, s32[8]{0:T(128)S(1)}, s32[]{:T(128)}, bf16[2,2,128,1024]{3,2,1,0:T(8,128)(2,1)S(1)}, /*index=5*/bf16[2...) while((s32[]{:T(128)}, f32[64,16384]{1,0:T(8,128)}, ...), condition=%wide.region_3.5_spmd.clone, body=%wide.region_0.4_spmd.clone.sunk | while | flops 585442176 | bytes 44893884 | solution.py:82
  429.7 11.7 add_reduce_fusion.6
  459.4 11.7 add_reduce_fusion.6
  489.2 11.7 add_reduce_fusion.6
  519.0 11.7 add_reduce_fusion.6
  548.8 11.7 add_reduce_fusion.6
  639.9 244.5 %while.41 = (s32[]{:T(128)}, f32[64,16384]{1,0:T(8,128)}, s32[8]{0:T(128)S(1)}, s32[]{:T(128)}, bf16[2,2,128,1024]{3,2,1,0:T(8,128)(2,1)}, /*index=5*/bf16[2,2,1...) while((s32[]{:T(128)}, f32[64,16384]{1,0:T(8,128)}, s32[8]{0:T(128)S(1)}, ...), condition=%wide.region_7.9_spmd.clone, body=%wide.region_4.8_spmd.clone.sunk | while | flops 585442176 | bytes 44893884 | solution.py:82
  642.4 11.7 add_reduce_fusion.7
  671.9 11.7 add_reduce_fusion.7
  702.6 11.7 add_reduce_fusion.7
  733.3 11.7 add_reduce_fusion.7
  764.0 11.7 add_reduce_fusion.7
  794.7 11.7 add_reduce_fusion.7
  825.4 11.7 add_reduce_fusion.7
  856.1 11.7 add_reduce_fusion.7
  889.0 243.9 %while.42 = (s32[]{:T(128)}, f32[64,16384]{1,0:T(8,128)}, s32[8]{0:T(128)S(1)}, s32[]{:T(128)}, bf16[2,2,128,1024]{3,2,1,0:T(8,128)(2,1)}, /*index=5*/bf16[2,2,1...) while((s32[]{:T(128)}, f32[64,16384]{1,0:T(8,128)}, s32[8]{0:T(128)S(1)}, ...), condition=%wide.region_11.13_spmd.clone, body=%wide.region_8.12_spmd.clone.sunk | while | flops 585442176 | bytes 44893884 | solution.py:82
  1147.2 45.3 %reduce-scatter.5.cloned.1.call-done = bf16[8,49152]{1,0:T(8,128)(2,1)} async-done(((bf16[64,49152]{1,0:T(8,128)(2,1)}), bf16[8,49152]{1,0:T(8,128)(2,1)}) %reduce-scatter.5.cloned.1.call-update) | async-done | bytes 786448
  (379 shorter events, 688.7 us)
Async XLA Ops:
  6.5 1186.0 %reduce-scatter.5.cloned.1.call-start = ((), (), s32[]{:S(2)}) async-start(), calls=%async_computation.1 | async-start | bytes 7077888
  6.5 52.6 %collective-permute-start = (bf16[2,2,2,128,1024]{4,3,2,1,0:T(8,128)(2,1)}, bf16[2,2,2,128,1024]{4,3,2,1,0:T(8,128)(2,1)S(1)}, u32[]{:S(2)}, u32[]{:S(2)}) collective-permute-start(bf16[2,2,2,128,1024]{4,3,2,1,0:T(8,128)(2,1)} %param.12), channel_id=1, source_target_pairs={{0,8},{8,16},{16,24},{24,32},{32,40},{40,48},{48,56},{56,64},{64,7... | collective-permute-start | bytes 6291464 | tf_op jit(solution)/shard_map/ppermute | solution.py:22
  9.0 50.1 %collective-permute-start.1 = (bf16[2,2,2,128,1024]{4,3,2,1,0:T(8,128)(2,1)}, bf16[2,2,2,128,1024]{4,3,2,1,0:T(8,128)(2,1)S(1)}, u32[]{:S(2)}, u32[]{:S(2)}) collective-permute-start(bf16[2,2,2,128,1024]{4,3,2,1,0:T(8,128)(2,1)} %param.12), channel_id=1, source_target_pairs={{0,120},{8,0},{16,8},{24,16},{32,24},{40,32},{48,40},{56,48},{64,5... | collective-permute-start | bytes 6291464 | tf_op jit(solution)/shard_map/ppermute | solution.py:27
  59.1 97.5 %copy-start.6 = (bf16[2,2,2,128,1024]{4,3,2,1,0:T(8,128)(2,1)}, bf16[2,2,2,128,1024]{4,3,2,1,0:T(8,128)(2,1)S(1)}, u32[]{:S(2)}) copy-start(bf16[2,2,2,128,1024]{4,3,2,1,0:T(8,128)(2,1)S(1)} %collective-permute-done) | copy-start | bytes 6291460
  59.1 49.2 %collective-permute-start.2 = (bf16[2,2,2,128,1024]{4,3,2,1,0:T(8,128)(2,1)S(1)}, bf16[2,2,2,128,1024]{4,3,2,1,0:T(8,128)(2,1)S(1)}, u32[]{:S(2)}, u32[]{:S(2)}) collective-permute-start(bf16[2,2,2,128,1024]{4,3,2,1,0:T(8,128)(2,1)S(1)} %collective-permute-done), channel_id=1, source_target_pairs={{0,8},{8,16},{16,24},{24,32},{32,40},{40,48},{48,56},{56,64},{64,7... | collective-permute-start | bytes 6291464 | tf_op jit(solution)/shard_map/ppermute | solution.py:22
  59.1 49.2 %collective-permute-start.3 = (bf16[2,2,2,128,1024]{4,3,2,1,0:T(8,128)(2,1)S(1)}, bf16[2,2,2,128,1024]{4,3,2,1,0:T(8,128)(2,1)S(1)}, u32[]{:S(2)}, u32[]{:S(2)}) collective-permute-start(bf16[2,2,2,128,1024]{4,3,2,1,0:T(8,128)(2,1)S(1)} %collective-permute-done.1), channel_id=1, source_target_pairs={{0,120},{8,0},{16,8},{24,16},{32,24},{40,32},{48,40},{56,48},{64,5... | collective-permute-start | bytes 6291464 | tf_op jit(solution)/shard_map/ppermute | solution.py:27
  108.4 48.3 %collective-permute-start.4 = (bf16[2,2,2,128,1024]{4,3,2,1,0:T(8,128)(2,1)S(1)}, bf16[2,2,2,128,1024]{4,3,2,1,0:T(8,128)(2,1)S(1)}, u32[]{:S(2)}, u32[]{:S(2)}) collective-permute-start(bf16[2,2,2,128,1024]{4,3,2,1,0:T(8,128)(2,1)S(1)} %collective-permute-done.2), channel_id=1, source_target_pairs={{0,8},{8,16},{16,24},{24,32},{32,40},{40,48},{48,56},{56,64},{64,7... | collective-permute-start | bytes 6291464 | tf_op jit(solution)/shard_map/ppermute | solution.py:22
  109.7 46.9 %copy-start.4 = (bf16[2,2,2,128,1024]{4,3,2,1,0:T(8,128)(2,1)}, bf16[2,2,2,128,1024]{4,3,2,1,0:T(8,128)(2,1)S(1)}, u32[]{:S(2)}) copy-start(bf16[2,2,2,128,1024]{4,3,2,1,0:T(8,128)(2,1)S(1)} %collective-permute-done.3) | copy-start | bytes 6291460
  109.7 46.9 %collective-permute-start.5 = (bf16[2,2,2,128,1024]{4,3,2,1,0:T(8,128)(2,1)S(1)}, bf16[2,2,2,128,1024]{4,3,2,1,0:T(8,128)(2,1)S(1)}, u32[]{:S(2)}, u32[]{:S(2)}) collective-permute-start(bf16[2,2,2,128,1024]{4,3,2,1,0:T(8,128)(2,1)S(1)} %collective-permute-done.3), channel_id=1, source_target_pairs={{0,120},{8,0},{16,8},{24,16},{32,24},{40,32},{48,40},{56,48},{64,5... | collective-permute-start | bytes 6291464 | tf_op jit(solution)/shard_map/ppermute | solution.py:27
  156.7 47.4 %collective-permute-start.6 = (bf16[2,2,2,128,1024]{4,3,2,1,0:T(8,128)(2,1)S(1)}, bf16[2,2,2,128,1024]{4,3,2,1,0:T(8,128)(2,1)S(1)}, u32[]{:S(2)}, u32[]{:S(2)}) collective-permute-start(bf16[2,2,2,128,1024]{4,3,2,1,0:T(8,128)(2,1)S(1)} %collective-permute-done.4), channel_id=1, source_target_pairs={{0,8},{8,16},{16,24},{24,32},{32,40},{40,48},{48,56},{56,64},{64,7... | collective-permute-start | bytes 6291464 | tf_op jit(solution)/shard_map/ppermute | solution.py:22
  156.7 47.3 %copy-start.10 = (bf16[2,2,2,128,1024]{4,3,2,1,0:T(8,128)(2,1)}, bf16[2,2,2,128,1024]{4,3,2,1,0:T(8,128)(2,1)S(1)}, u32[]{:S(2)}) copy-start(bf16[2,2,2,128,1024]{4,3,2,1,0:T(8,128)(2,1)S(1)} %collective-permute-done.5) | copy-start | bytes 6291460
  156.7 47.3 %collective-permute-start.7 = (bf16[2,2,2,128,1024]{4,3,2,1,0:T(8,128)(2,1)S(1)}, bf16[2,2,2,128,1024]{4,3,2,1,0:T(8,128)(2,1)S(1)}, u32[]{:S(2)}, u32[]{:S(2)}) collective-permute-start(bf16[2,2,2,128,1024]{4,3,2,1,0:T(8,128)(2,1)S(1)} %collective-permute-done.5), channel_id=1, source_target_pairs={{0,120},{8,0},{16,8},{24,16},{32,24},{40,32},{48,40},{56,48},{64,5... | collective-permute-start | bytes 6291464 | tf_op jit(solution)/shard_map/ppermute | solution.py:27
  204.0 46.5 %collective-permute-start.8 = (bf16[2,2,2,128,1024]{4,3,2,1,0:T(8,128)(2,1)S(1)}, bf16[2,2,2,128,1024]{4,3,2,1,0:T(8,128)(2,1)S(1)}, u32[]{:S(2)}, u32[]{:S(2)}) collective-permute-start(bf16[2,2,2,128,1024]{4,3,2,1,0:T(8,128)(2,1)S(1)} %collective-permute-done.6), channel_id=1, source_target_pairs={{0,8},{8,16},{16,24},{24,32},{32,40},{40,48},{48,56},{56,64},{64,7... | collective-permute-start | bytes 6291464 | tf_op jit(solution)/shard_map/ppermute | solution.py:22
  205.4 45.1 %copy-start.14 = (bf16[2,2,2,128,1024]{4,3,2,1,0:T(8,128)(2,1)}, bf16[2,2,2,128,1024]{4,3,2,1,0:T(8,128)(2,1)S(1)}, u32[]{:S(2)}) copy-start(bf16[2,2,2,128,1024]{4,3,2,1,0:T(8,128)(2,1)S(1)} %collective-permute-done.7) | copy-start | bytes 6291460
  205.4 45.1 %collective-permute-start.9 = (bf16[2,2,2,128,1024]{4,3,2,1,0:T(8,128)(2,1)S(1)}, bf16[2,2,2,128,1024]{4,3,2,1,0:T(8,128)(2,1)}, u32[]{:S(2)}, u32[]{:S(2)}) collective-permute-start(bf16[2,2,2,128,1024]{4,3,2,1,0:T(8,128)(2,1)S(1)} %collective-permute-done.7), channel_id=1, source_target_pairs={{0,120},{8,0},{16,8},{24,16},{32,24},{40,32},{48,40},{56,48},{64,5... | collective-permute-start | bytes 6291464 | tf_op jit(solution)/shard_map/ppermute | solution.py:27
  250.5 45.6 %collective-permute-start.10 = (bf16[2,2,2,128,1024]{4,3,2,1,0:T(8,128)(2,1)S(1)}, bf16[2,2,2,128,1024]{4,3,2,1,0:T(8,128)(2,1)}, u32[]{:S(2)}, u32[]{:S(2)}) collective-permute-start(bf16[2,2,2,128,1024]{4,3,2,1,0:T(8,128)(2,1)S(1)} %collective-permute-done.8), channel_id=1, source_target_pairs={{0,8},{8,16},{16,24},{24,32},{32,40},{40,48},{48,56},{56,64},{64,7... | collective-permute-start | bytes 6291464 | tf_op jit(solution)/shard_map/ppermute | solution.py:22
  251.8 72.6 %collective-permute-start.11 = (bf16[2,2,2,128,1024]{4,3,2,1,0:T(8,128)(2,1)}, bf16[2,2,2,128,1024]{4,3,2,1,0:T(8,128)(2,1)}, u32[]{:S(2)}, u32[]{:S(2)}) collective-permute-start(bf16[2,2,2,128,1024]{4,3,2,1,0:T(8,128)(2,1)} %collective-permute-done.9), channel_id=1, source_target_pairs={{0,120},{8,0},{16,8},{24,16},{32,24},{40,32},{48,40},{56,48},{64,5... | collective-permute-start | bytes 6291464 | tf_op jit(solution)/shard_map/ppermute | solution.py:27
  296.1 44.9 %collective-permute-start.12 = (bf16[2,2,2,128,1024]{4,3,2,1,0:T(8,128)(2,1)}, bf16[2,2,2,128,1024]{4,3,2,1,0:T(8,128)(2,1)}, u32[]{:S(2)}, u32[]{:S(2)}) collective-permute-start(bf16[2,2,2,128,1024]{4,3,2,1,0:T(8,128)(2,1)} %collective-permute-done.10), channel_id=1, source_target_pairs={{0,8},{8,16},{16,24},{24,32},{32,40},{40,48},{48,56},{56,64},{64,7... | collective-permute-start | bytes 6291464 | tf_op jit(solution)/shard_map/ppermute | solution.py:22
  311.2 18.0 %copy-start.7 = (bf16[2,2,2,128,1024]{4,3,2,1,0:T(8,128)(2,1)S(1)}, bf16[2,2,2,128,1024]{4,3,2,1,0:T(8,128)(2,1)}, u32[]{:S(2)}) copy-start(bf16[2,2,2,128,1024]{4,3,2,1,0:T(8,128)(2,1)} %copy-done.6) | copy-start | bytes 6291460
  322.8 19.8 %copy-start.3 = (bf16[2,2,2,128,1024]{4,3,2,1,0:T(8,128)(2,1)S(1)}, bf16[2,2,2,128,1024]{4,3,2,1,0:T(8,128)(2,1)}, u32[]{:S(2)}) copy-start(bf16[2,2,2,128,1024]{4,3,2,1,0:T(8,128)(2,1)} %copy-done.2) | copy-start | bytes 6291460
  324.4 19.8 %copy-start.5 = (bf16[2,2,2,128,1024]{4,3,2,1,0:T(8,128)(2,1)S(1)}, bf16[2,2,2,128,1024]{4,3,2,1,0:T(8,128)(2,1)}, u32[]{:S(2)}) copy-start(bf16[2,2,2,128,1024]{4,3,2,1,0:T(8,128)(2,1)} %copy-done.4) | copy-start | bytes 6291460
  324.4 44.0 %collective-permute-start.13 = (bf16[2,2,2,128,1024]{4,3,2,1,0:T(8,128)(2,1)}, bf16[2,2,2,128,1024]{4,3,2,1,0:T(8,128)(2,1)S(1)}, u32[]{:S(2)}, u32[]{:S(2)}) collective-permute-start(bf16[2,2,2,128,1024]{4,3,2,1,0:T(8,128)(2,1)} %collective-permute-done.11), channel_id=1, source_target_pairs={{0,120},{8,0},{16,8},{24,16},{32,24},{40,32},{48,40},{56,48},{64,5... | collective-permute-start | bytes 6291464 | tf_op jit(solution)/shard_map/ppermute | solution.py:27
  330.7 15.0 %copy-start.9 = (bf16[2,2,2,128,1024]{4,3,2,1,0:T(8,128)(2,1)S(1)}, bf16[2,2,2,128,1024]{4,3,2,1,0:T(8,128)(2,1)}, u32[]{:S(2)}) copy-start(bf16[2,2,2,128,1024]{4,3,2,1,0:T(8,128)(2,1)} %copy-done.8) | copy-start | bytes 6291460
  341.0 43.9 %collective-permute-start.14 = (bf16[2,2,2,128,1024]{4,3,2,1,0:T(8,128)(2,1)}, bf16[2,2,2,128,1024]{4,3,2,1,0:T(8,128)(2,1)S(1)}, u32[]{:S(2)}, u32[]{:S(2)}) collective-permute-start(bf16[2,2,2,128,1024]{4,3,2,1,0:T(8,128)(2,1)} %collective-permute-done.12), channel_id=1, source_target_pairs={{0,8},{8,16},{16,24},{24,32},{32,40},{40,48},{48,56},{56,64},{64,7... | collective-permute-start | bytes 6291464 | tf_op jit(solution)/shard_map/ppermute | solution.py:22
  (10 other events, 42.5 us)
Sparse Core Ops, SparseCore 0:
  1147.3 45.1 reduce-scatter.4
